TPU v7x, 32 devices: a whole 2x2x4 slice. The times are simulated.
32 devices in a mesh: grp: 4 (over x, core), row: 8 (over z, y).
Axes of the slice: x: 2, y: 2, z: 4, core: 2. Of those that a mesh axis runs over, the one named last changes fastest.
Arguments:
- features: bfloat16 [2048, 4096], P('row', 'grp'), may hold values from -0.125 to 0.125
- residual: float32 [2048, 576], P('row'), may hold values from -6 to 6
- precond: float32 [4096, 1024], P('grp'), as said below
Outputs:
- coefs: float32 [4096, 576], P('grp')
- section_resid: float32 [4, 2048, 576], P('grp', 'row')
Inputs may be any that keep to these rules, and one draw needn't show every extreme that they name: Each 1024 x 1024 block of precond is symmetric and positive definite.
All inputs are finite; a program needn't handle non-finite values.
Results may differ from a plain program's by a relative error of at most 0.009.
Values may be sent and summed in bfloat16 or wider, within the bound.
No kernel may reach another device: no remote copies, remote signals or barrier semaphores. Data moves between devices by JAX's collectives and lax.ppermute only.
A program may use at most 64 MiB of HBM per device.

v0:
```python
import jax
import jax.numpy as jnp
from jax import lax
from jax.sharding import PartitionSpec as P


def from_behind(block, axis, distance):
    devices = range(lax.axis_size(axis))
    route = [(i - distance, i) for i in devices if i - distance in devices]
    return lax.ppermute(block, axis, route)


def chain_sweep(features, residual, precond):
    section_index = lax.axis_index("grp")
    section_count = lax.axis_size("grp")
    row_count, target_width = residual.shape
    block_width = features.shape[1]
    panel_count = 3
    panel_width = target_width // panel_count
    step_count = section_count + panel_count - 1

    def correlate(rounded):
        correlation = lax.dot_general(
            features, rounded, (((0,), (0,)), ((), ())), preferred_element_type=jnp.float32
        )
        correlation = lax.psum(correlation, "row")
        return jnp.dot(precond, correlation, precision=lax.Precision.HIGHEST)

    def turn(turn_index, loop_state):
        current, coef_table, resid_table = loop_state
        position = turn_index - section_index
        inside = jnp.logical_and(position >= 0, position < panel_count)
        panel_slot = jnp.clip(position, 0, panel_count - 1) * panel_width
        fresh_panel = lax.dynamic_slice_in_dim(residual, panel_slot, panel_width, 1)
        current = jnp.where(section_index == 0, fresh_panel, current)
        rounded = current.astype(jnp.bfloat16)
        coefficient = correlate(rounded)
        updated = current - jnp.dot(
            features, coefficient.astype(jnp.bfloat16), preferred_element_type=jnp.float32
        )
        old_coef = lax.dynamic_slice_in_dim(coef_table, panel_slot, panel_width, 1)
        coef_table = lax.dynamic_update_slice_in_dim(
            coef_table, jnp.where(inside, coefficient, old_coef), panel_slot, 1
        )
        old_resid = lax.dynamic_slice_in_dim(resid_table, panel_slot, panel_width, 2)
        resid_table = lax.dynamic_update_slice_in_dim(
            resid_table, jnp.where(inside, updated[None], old_resid), panel_slot, 2
        )
        passed = from_behind(updated, "grp", 1)
        return (passed, coef_table, resid_table)

    start_state = (
        jnp.zeros((row_count, panel_width), jnp.float32),
        jnp.zeros((block_width, target_width), jnp.float32),
        jnp.zeros((1, row_count, target_width), jnp.float32),
    )
    final_state = lax.fori_loop(0, step_count, turn, start_state)
    return (final_state[1], final_state[2])


def local(features, residual, precond):
    return chain_sweep(features, residual, precond)


def solution(mesh):
    placed = (P("row", "grp"), P("row", None), P("grp", None))
    return jax.shard_map(
        local,
        mesh=mesh,
        in_specs=placed,
        out_specs=(P("grp", None), P("grp", "row", None)),
        check_vma=False,
    )
```

profile of v0, /device:TPU:1, one launch (start us, length us, event | category | flops | bytes accessed | tf_op | source)
XLA Modules:
  0.0 584.3 jit_solution(12787085232364067102)
XLA Ops:
  8.3 567.7 %while.18 = (s32[]{:T(128)}, f32[256,192]{0,1:T(8,128)S(1)}, f32[1024,576]{0,1:T(8,128)S(1)}, f32[1,256,576]{1,2,0:T(8,128)}, pred[]{:T(512)}, /*index=5*/s32[]{...) while((s32[]{:T(128)}, f32[256,192]{0,1:T(8,128)S(1)}, ...), condition=%wide.region_2.3_spmd, body=%wide.region_0.2_spmd.sunk | while | flops 2618032128 | bytes 20677516 | solution.py:57
  10.5 78.6 %all-reduce.2.cloned.1.call-done = f32[1024,192]{0,1:T(8,128)} async-done(((f32[1024,192]{0,1:T(8,128)}), f32[1024,192]{0,1:T(8,128)}) %all-reduce.2.cloned.1.call-update) | async-done | bytes 786448 | tf_op jit(solution)/shard_map/while/body/eval_jaxpr/psum | solution.py:26
  89.2 6.3 %select_dynamic-update-slice_fusion.2 = (f32[1024,576]{0,1:T(8,128)S(1)}, bf16[1024,192]{0,1:T(8,128)(2,1)S(1)}) fusion(f32[1024,576]{0,1:T(8,128)S(1)} %get-tuple-element.285, s32[]{:T(128)S(6)} %select_n.97, pred[]{:T(512)S(6)} %and.10, f32[1024,192]{0,1:T(8,128)} %all-reduce.2.cloned.1.call-done, f32[1024,1024]{1,0:T(8,128)} %get-tuple-element.306), kind=kOutput, calls=%fused_computation.4.clone.1 | convolution fusion | flops 2416312320 | bytes 6946821 | tf_op jit(solution)/shard_map/while/body/eval_jaxpr/dot_general | solution.py:27
  97.6 4.8 collective-permute-start
  102.4 2.6 collective-permute-done
  107.1 76.5 %all-reduce.2.cloned.1.call-done = f32[1024,192]{0,1:T(8,128)} async-done(((f32[1024,192]{0,1:T(8,128)}), f32[1024,192]{0,1:T(8,128)}) %all-reduce.2.cloned.1.call-update) | async-done | bytes 786448 | tf_op jit(solution)/shard_map/while/body/eval_jaxpr/psum | solution.py:26
  183.6 6.3 %select_dynamic-update-slice_fusion.2 = (f32[1024,576]{0,1:T(8,128)S(1)}, bf16[1024,192]{0,1:T(8,128)(2,1)S(1)}) fusion(f32[1024,576]{0,1:T(8,128)S(1)} %get-tuple-element.285, s32[]{:T(128)S(6)} %select_n.97, pred[]{:T(512)S(6)} %and.10, f32[1024,192]{0,1:T(8,128)} %all-reduce.2.cloned.1.call-done, f32[1024,1024]{1,0:T(8,128)} %get-tuple-element.306), kind=kOutput, calls=%fused_computation.4.clone.1 | convolution fusion | flops 2416312320 | bytes 6946821 | tf_op jit(solution)/shard_map/while/body/eval_jaxpr/dot_general | solution.py:27
  192.0 4.8 collective-permute-start
  196.8 2.6 collective-permute-done
  201.5 76.5 %all-reduce.2.cloned.1.call-done = f32[1024,192]{0,1:T(8,128)} async-done(((f32[1024,192]{0,1:T(8,128)}), f32[1024,192]{0,1:T(8,128)}) %all-reduce.2.cloned.1.call-update) | async-done | bytes 786448 | tf_op jit(solution)/shard_map/while/body/eval_jaxpr/psum | solution.py:26
  278.0 6.3 %select_dynamic-update-slice_fusion.2 = (f32[1024,576]{0,1:T(8,128)S(1)}, bf16[1024,192]{0,1:T(8,128)(2,1)S(1)}) fusion(f32[1024,576]{0,1:T(8,128)S(1)} %get-tuple-element.285, s32[]{:T(128)S(6)} %select_n.97, pred[]{:T(512)S(6)} %and.10, f32[1024,192]{0,1:T(8,128)} %all-reduce.2.cloned.1.call-done, f32[1024,1024]{1,0:T(8,128)} %get-tuple-element.306), kind=kOutput, calls=%fused_computation.4.clone.1 | convolution fusion | flops 2416312320 | bytes 6946821 | tf_op jit(solution)/shard_map/while/body/eval_jaxpr/dot_general | solution.py:27
  286.4 4.8 collective-permute-start
  291.3 2.6 collective-permute-done
  296.0 76.1 %all-reduce.2.cloned.1.call-done = f32[1024,192]{0,1:T(8,128)} async-done(((f32[1024,192]{0,1:T(8,128)}), f32[1024,192]{0,1:T(8,128)}) %all-reduce.2.cloned.1.call-update) | async-done | bytes 786448 | tf_op jit(solution)/shard_map/while/body/eval_jaxpr/psum | solution.py:26
  372.1 6.3 %select_dynamic-update-slice_fusion.2 = (f32[1024,576]{0,1:T(8,128)S(1)}, bf16[1024,192]{0,1:T(8,128)(2,1)S(1)}) fusion(f32[1024,576]{0,1:T(8,128)S(1)} %get-tuple-element.285, s32[]{:T(128)S(6)} %select_n.97, pred[]{:T(512)S(6)} %and.10, f32[1024,192]{0,1:T(8,128)} %all-reduce.2.cloned.1.call-done, f32[1024,1024]{1,0:T(8,128)} %get-tuple-element.306), kind=kOutput, calls=%fused_computation.4.clone.1 | convolution fusion | flops 2416312320 | bytes 6946821 | tf_op jit(solution)/shard_map/while/body/eval_jaxpr/dot_general | solution.py:27
  380.5 4.8 collective-permute-start
  390.1 76.1 %all-reduce.2.cloned.1.call-done = f32[1024,192]{0,1:T(8,128)} async-done(((f32[1024,192]{0,1:T(8,128)}), f32[1024,192]{0,1:T(8,128)}) %all-reduce.2.cloned.1.call-update) | async-done | bytes 786448 | tf_op jit(solution)/shard_map/while/body/eval_jaxpr/psum | solution.py:26
  466.1 6.3 %select_dynamic-update-slice_fusion.2 = (f32[1024,576]{0,1:T(8,128)S(1)}, bf16[1024,192]{0,1:T(8,128)(2,1)S(1)}) fusion(f32[1024,576]{0,1:T(8,128)S(1)} %get-tuple-element.285, s32[]{:T(128)S(6)} %select_n.97, pred[]{:T(512)S(6)} %and.10, f32[1024,192]{0,1:T(8,128)} %all-reduce.2.cloned.1.call-done, f32[1024,1024]{1,0:T(8,128)} %get-tuple-element.306), kind=kOutput, calls=%fused_computation.4.clone.1 | convolution fusion | flops 2416312320 | bytes 6946821 | tf_op jit(solution)/shard_map/while/body/eval_jaxpr/dot_general | solution.py:27
  474.5 4.8 collective-permute-start
  479.4 2.6 collective-permute-done
  484.1 76.1 %all-reduce.2.cloned.1.call-done = f32[1024,192]{0,1:T(8,128)} async-done(((f32[1024,192]{0,1:T(8,128)}), f32[1024,192]{0,1:T(8,128)}) %all-reduce.2.cloned.1.call-update) | async-done | bytes 786448 | tf_op jit(solution)/shard_map/while/body/eval_jaxpr/psum | solution.py:26
  560.2 6.3 %select_dynamic-update-slice_fusion.2 = (f32[1024,576]{0,1:T(8,128)S(1)}, bf16[1024,192]{0,1:T(8,128)(2,1)S(1)}) fusion(f32[1024,576]{0,1:T(8,128)S(1)} %get-tuple-element.285, s32[]{:T(128)S(6)} %select_n.97, pred[]{:T(512)S(6)} %and.10, f32[1024,192]{0,1:T(8,128)} %all-reduce.2.cloned.1.call-done, f32[1024,1024]{1,0:T(8,128)} %get-tuple-element.306), kind=kOutput, calls=%fused_computation.4.clone.1 | convolution fusion | flops 2416312320 | bytes 6946821 | tf_op jit(solution)/shard_map/while/body/eval_jaxpr/dot_general | solution.py:27
  568.6 4.8 collective-permute-start
  573.4 2.6 collective-permute-done
  (56 shorter events, 30.2 us)
Async XLA Ops:
  7.2 1.2 copy-start
  8.4 80.8 %all-reduce.2.cloned.1.call-start = ((), (), s32[]{:S(2)}) async-start(), calls=%async_computation | async-start | bytes 1572864 | tf_op jit(solution)/shard_map/while/body/eval_jaxpr/psum | solution.py:26
  89.2 6.3 %copy-start.2 = (f32[1,256,576]{1,2,0:T(8,128)S(1)}, f32[1,256,576]{1,2,0:T(8,128)}, u32[]{:S(2)}) copy-start(f32[1,256,576]{1,2,0:T(8,128)} %get-tuple-element.286) | copy-start | bytes 1769476 | tf_op jit(solution)/shard_map/while
  96.7 0.8 copy-start.3
  97.6 7.4 %collective-permute-start = (f32[256,192]{0,1:T(8,128)S(1)}, f32[256,192]{0,1:T(8,128)S(1)}, u32[]{:S(2)}, u32[]{:S(2)}) collective-permute-start(f32[256,192]{0,1:T(8,128)S(1)} %get-tuple-element.265), channel_id=1, source_target_pairs={{0,8},{8,16},{16,24},{1,9},{9,17},{17,25},{2,10},{10,18},{18,26},{... | collective-permute-start | bytes 589832 | tf_op jit(solution)/shard_map/while/body/eval_jaxpr/ppermute | solution.py:10
  105.0 78.6 %all-reduce.2.cloned.1.call-start = ((), (), s32[]{:S(2)}) async-start(), calls=%async_computation | async-start | bytes 1572864 | tf_op jit(solution)/shard_map/while/body/eval_jaxpr/psum | solution.py:26
  183.6 6.3 %copy-start.2 = (f32[1,256,576]{1,2,0:T(8,128)S(1)}, f32[1,256,576]{1,2,0:T(8,128)}, u32[]{:S(2)}) copy-start(f32[1,256,576]{1,2,0:T(8,128)} %get-tuple-element.286) | copy-start | bytes 1769476 | tf_op jit(solution)/shard_map/while
  191.2 0.8 copy-start.3
  192.0 7.4 %collective-permute-start = (f32[256,192]{0,1:T(8,128)S(1)}, f32[256,192]{0,1:T(8,128)S(1)}, u32[]{:S(2)}, u32[]{:S(2)}) collective-permute-start(f32[256,192]{0,1:T(8,128)S(1)} %get-tuple-element.265), channel_id=1, source_target_pairs={{0,8},{8,16},{16,24},{1,9},{9,17},{17,25},{2,10},{10,18},{18,26},{... | collective-permute-start | bytes 589832 | tf_op jit(solution)/shard_map/while/body/eval_jaxpr/ppermute | solution.py:10
  199.4 78.6 %all-reduce.2.cloned.1.call-start = ((), (), s32[]{:S(2)}) async-start(), calls=%async_computation | async-start | bytes 1572864 | tf_op jit(solution)/shard_map/while/body/eval_jaxpr/psum | solution.py:26
  278.0 6.3 %copy-start.2 = (f32[1,256,576]{1,2,0:T(8,128)S(1)}, f32[1,256,576]{1,2,0:T(8,128)}, u32[]{:S(2)}) copy-start(f32[1,256,576]{1,2,0:T(8,128)} %get-tuple-element.286) | copy-start | bytes 1769476 | tf_op jit(solution)/shard_map/while
  285.6 0.8 copy-start.3
  286.4 7.4 %collective-permute-start = (f32[256,192]{0,1:T(8,128)S(1)}, f32[256,192]{0,1:T(8,128)S(1)}, u32[]{:S(2)}, u32[]{:S(2)}) collective-permute-start(f32[256,192]{0,1:T(8,128)S(1)} %get-tuple-element.265), channel_id=1, source_target_pairs={{0,8},{8,16},{16,24},{1,9},{9,17},{17,25},{2,10},{10,18},{18,26},{... | collective-permute-start | bytes 589832 | tf_op jit(solution)/shard_map/while/body/eval_jaxpr/ppermute | solution.py:10
  293.9 78.2 %all-reduce.2.cloned.1.call-start = ((), (), s32[]{:S(2)}) async-start(), calls=%async_computation | async-start | bytes 1572864 | tf_op jit(solution)/shard_map/while/body/eval_jaxpr/psum | solution.py:26
  372.1 6.3 %copy-start.2 = (f32[1,256,576]{1,2,0:T(8,128)S(1)}, f32[1,256,576]{1,2,0:T(8,128)}, u32[]{:S(2)}) copy-start(f32[1,256,576]{1,2,0:T(8,128)} %get-tuple-element.286) | copy-start | bytes 1769476 | tf_op jit(solution)/shard_map/while
  379.7 0.8 copy-start.3
  380.5 7.4 %collective-permute-start = (f32[256,192]{0,1:T(8,128)S(1)}, f32[256,192]{0,1:T(8,128)S(1)}, u32[]{:S(2)}, u32[]{:S(2)}) collective-permute-start(f32[256,192]{0,1:T(8,128)S(1)} %get-tuple-element.265), channel_id=1, source_target_pairs={{0,8},{8,16},{16,24},{1,9},{9,17},{17,25},{2,10},{10,18},{18,26},{... | collective-permute-start | bytes 589832 | tf_op jit(solution)/shard_map/while/body/eval_jaxpr/ppermute | solution.py:10
  387.9 78.2 %all-reduce.2.cloned.1.call-start = ((), (), s32[]{:S(2)}) async-start(), calls=%async_computation | async-start | bytes 1572864 | tf_op jit(solution)/shard_map/while/body/eval_jaxpr/psum | solution.py:26
  466.1 6.3 %copy-start.2 = (f32[1,256,576]{1,2,0:T(8,128)S(1)}, f32[1,256,576]{1,2,0:T(8,128)}, u32[]{:S(2)}) copy-start(f32[1,256,576]{1,2,0:T(8,128)} %get-tuple-element.286) | copy-start | bytes 1769476 | tf_op jit(solution)/shard_map/while
  474.5 7.4 %collective-permute-start = (f32[256,192]{0,1:T(8,128)S(1)}, f32[256,192]{0,1:T(8,128)S(1)}, u32[]{:S(2)}, u32[]{:S(2)}) collective-permute-start(f32[256,192]{0,1:T(8,128)S(1)} %get-tuple-element.265), channel_id=1, source_target_pairs={{0,8},{8,16},{16,24},{1,9},{9,17},{17,25},{2,10},{10,18},{18,26},{... | collective-permute-start | bytes 589832 | tf_op jit(solution)/shard_map/while/body/eval_jaxpr/ppermute | solution.py:10
  482.0 78.2 %all-reduce.2.cloned.1.call-start = ((), (), s32[]{:S(2)}) async-start(), calls=%async_computation | async-start | bytes 1572864 | tf_op jit(solution)/shard_map/while/body/eval_jaxpr/psum | solution.py:26
  560.2 6.3 %copy-start.2 = (f32[1,256,576]{1,2,0:T(8,128)S(1)}, f32[1,256,576]{1,2,0:T(8,128)}, u32[]{:S(2)}) copy-start(f32[1,256,576]{1,2,0:T(8,128)} %get-tuple-element.286) | copy-start | bytes 1769476 | tf_op jit(solution)/shard_map/while
  568.6 7.4 %collective-permute-start = (f32[256,192]{0,1:T(8,128)S(1)}, f32[256,192]{0,1:T(8,128)S(1)}, u32[]{:S(2)}, u32[]{:S(2)}) collective-permute-start(f32[256,192]{0,1:T(8,128)S(1)} %get-tuple-element.265), channel_id=1, source_target_pairs={{0,8},{8,16},{16,24},{1,9},{9,17},{17,25},{2,10},{10,18},{18,26},{... | collective-permute-start | bytes 589832 | tf_op jit(solution)/shard_map/while/body/eval_jaxpr/ppermute | solution.py:10
  576.0 1.4 copy-start.1
  (2 other events, 1.6 us)
Sparse Core Ops, SparseCore 0:
  13.2 75.9 all-reduce.1
  109.8 73.7 all-reduce.1
  204.2 73.7 all-reduce.1
  298.3 73.7 all-reduce.1
  392.4 73.6 all-reduce.1
  486.4 73.6 all-reduce.1
where the time goes:
time: 585 us; the launch traced here: 584 us
  waiting for transfers between devices  475 us (81%)
  matrix products  57.9 us (10%)
  starting transfers between devices  29 us (5%)
  between operations  14 us (2%)
  local copies, waits for them, and re-layouts  7.44 us (1%)
    psum x6, waiting for transfers between devices, correlate(): correlation = lax.psum(correlation, 'row')  460 us
    dot_general x6, matrix products, correlate(): return jnp.dot(precond, correlation, precision=lax.Precision.HIGHEST)  37.8 us
    ppermute x6, starting transfers between devices, from_behind(): return lax.ppermute(block, axis, route)  29 us
    ppermute x6, waiting for transfers between devices, from_behind(): return lax.ppermute(block, axis, route)  15.5 us
    dot_general x6, matrix products, correlate(): lax.dot_general(features, rounded, (((0,), (0,)), ((), ())), preferred_el...  12.5 us
  transfers between devices with their start and end apart: 12, of which 12 were waited for; matrix products, arithmetic and copies ran while one was open for 0% of the time, Pallas kernels for 0%

commit v1 on v0

--- a/solution.py
+++ b/solution.py
@@ -23,7 +23,7 @@
         correlation = lax.dot_general(
             features, rounded, (((0,), (0,)), ((), ())), preferred_element_type=jnp.float32
         )
-        correlation = lax.psum(correlation, "row")
+        correlation = jnp.sum(lax.all_gather(correlation, "row"), axis=0)
         return jnp.dot(precond, correlation, precision=lax.Precision.HIGHEST)
 
     def turn(turn_index, loop_state):

time: 585 us -> 760 us (1.30)
  waiting for transfers between devices: 475 us -> 603 us
  local copies, waits for them, and re-layouts: 7.44 us -> 55 us
  matrix products: 57.9 us -> 47.7 us
  other arithmetic: 0 us -> 9.07 us
    all_gather x0 -> x6, waiting for transfers between devices: none -> 587 us  [correlate(): correlation = jnp.sum(lax.all_gather(correlation, 'row'), axis=0)]
    psum x6 -> x0, waiting for transfers between devices: 460 us -> none  [correlate(): correlation = lax.psum(correlation, 'row')]
    while x24 -> x30, local copies, waits for them, and re-layouts: 4.88 us -> 53.1 us
    dot_general x6, matrix products: 37.8 us -> 26.3 us  [correlate(): return jnp.dot(precond, correlation, precision=lax.Precision.HIGHEST)]
    reduce_sum x0 -> x6, other arithmetic: none -> 9.07 us  [correlate(): correlation = jnp.sum(lax.all_gather(correlation, 'row'), axis=0)]
where the time goes in v1:
time: 760 us; the launch traced here: 759 us
  waiting for transfers between devices  603 us (79%)
  local copies, waits for them, and re-layouts  55 us (7%)
  matrix products  47.7 us (6%)
  starting transfers between devices  30.1 us (4%)
  between operations  14 us (2%)
  other arithmetic  9.07 us (1%)
    all_gather x6, waiting for transfers between devices, correlate(): correlation = jnp.sum(lax.all_gather(correlation, 'row'), axis=0)  587 us
    while x30, local copies, waits for them, and re-layouts  53.1 us
    ppermute x6, starting transfers between devices, from_behind(): return lax.ppermute(block, axis, route)  30 us
    dot_general x6, matrix products, correlate(): return jnp.dot(precond, correlation, precision=lax.Precision.HIGHEST)  26.3 us
    ppermute x6, waiting for transfers between devices, from_behind(): return lax.ppermute(block, axis, route)  15.5 us
  transfers between devices with their start and end apart: 12, of which 12 were waited for; matrix products, arithmetic and copies ran while one was open for 0% of the time, Pallas kernels for 0%

profile of v1, /device:TPU:1, one launch (start us, length us, event | category | flops | bytes accessed | tf_op | source)
XLA Modules:
  0.0 759.3 jit_solution(12378075118462691362)
XLA Ops:
  7.5 743.4 %while.18 = (s32[]{:T(128)}, f32[256,192]{0,1:T(8,128)S(1)}, f32[1024,576]{0,1:T(8,128)S(1)}, f32[1,256,576]{1,2,0:T(8,128)S(1)}, pred[]{:T(512)}, /*index=5*/s3...) while((s32[]{:T(128)}, f32[256,192]{0,1:T(8,128)S(1)}, ...), condition=%wide.region_2.3_spmd, body=%wide.region_0.2_spmd.sunk | while | flops 2619211776 | bytes 71009168 | solution.py:57
  9.9 100.6 %all-gather.5.cloned.1.call-done = f32[8192,192]{0,1:T(8,128)} async-done(((f32[1024,192]{0,1:T(8,128)}), f32[8192,192]{0,1:T(8,128)}) %all-gather.5.cloned.1.call-update) | async-done | bytes 6291472 | tf_op jit(solution)/shard_map/while/body/eval_jaxpr/all_gather | solution.py:26
  110.6 8.2 %copy.7 = f32[24,8,8,1024]{3,2,1,0:T(8,128)S(1)} copy(f32[24,8,8,1024]{3,1,2,0:T(8,128)} %bitcast.40) | data formatting | bytes 12582912 | tf_op jit(solution)/shard_map/while
  120.9 4.4 select_dynamic-update-slice_fusion.2
  126.6 5.0 collective-permute-start
  136.6 97.5 %all-gather.5.cloned.1.call-done = f32[8192,192]{0,1:T(8,128)} async-done(((f32[1024,192]{0,1:T(8,128)}), f32[8192,192]{0,1:T(8,128)}) %all-gather.5.cloned.1.call-update) | async-done | bytes 6291472 | tf_op jit(solution)/shard_map/while/body/eval_jaxpr/all_gather | solution.py:26
  234.1 8.2 %copy.7 = f32[24,8,8,1024]{3,2,1,0:T(8,128)S(1)} copy(f32[24,8,8,1024]{3,1,2,0:T(8,128)} %bitcast.40) | data formatting | bytes 12582912 | tf_op jit(solution)/shard_map/while
  244.5 4.4 select_dynamic-update-slice_fusion.2
  250.2 5.0 collective-permute-start
  260.1 97.5 %all-gather.5.cloned.1.call-done = f32[8192,192]{0,1:T(8,128)} async-done(((f32[1024,192]{0,1:T(8,128)}), f32[8192,192]{0,1:T(8,128)}) %all-gather.5.cloned.1.call-update) | async-done | bytes 6291472 | tf_op jit(solution)/shard_map/while/body/eval_jaxpr/all_gather | solution.py:26
  357.6 8.2 %copy.7 = f32[24,8,8,1024]{3,2,1,0:T(8,128)S(1)} copy(f32[24,8,8,1024]{3,1,2,0:T(8,128)} %bitcast.40) | data formatting | bytes 12582912 | tf_op jit(solution)/shard_map/while
  368.0 4.4 select_dynamic-update-slice_fusion.2
  373.7 5.0 collective-permute-start
  383.6 97.2 %all-gather.5.cloned.1.call-done = f32[8192,192]{0,1:T(8,128)} async-done(((f32[1024,192]{0,1:T(8,128)}), f32[8192,192]{0,1:T(8,128)}) %all-gather.5.cloned.1.call-update) | async-done | bytes 6291472 | tf_op jit(solution)/shard_map/while/body/eval_jaxpr/all_gather | solution.py:26
  480.8 8.2 %copy.7 = f32[24,8,8,1024]{3,2,1,0:T(8,128)S(1)} copy(f32[24,8,8,1024]{3,1,2,0:T(8,128)} %bitcast.40) | data formatting | bytes 12582912 | tf_op jit(solution)/shard_map/while
  491.2 4.4 select_dynamic-update-slice_fusion.2
  496.9 5.0 collective-permute-start
  506.8 97.2 %all-gather.5.cloned.1.call-done = f32[8192,192]{0,1:T(8,128)} async-done(((f32[1024,192]{0,1:T(8,128)}), f32[8192,192]{0,1:T(8,128)}) %all-gather.5.cloned.1.call-update) | async-done | bytes 6291472 | tf_op jit(solution)/shard_map/while/body/eval_jaxpr/all_gather | solution.py:26
  604.0 8.2 %copy.7 = f32[24,8,8,1024]{3,2,1,0:T(8,128)S(1)} copy(f32[24,8,8,1024]{3,1,2,0:T(8,128)} %bitcast.40) | data formatting | bytes 12582912 | tf_op jit(solution)/shard_map/while
  620.1 5.0 collective-permute-start
  630.0 97.2 %all-gather.5.cloned.1.call-done = f32[8192,192]{0,1:T(8,128)} async-done(((f32[1024,192]{0,1:T(8,128)}), f32[8192,192]{0,1:T(8,128)}) %all-gather.5.cloned.1.call-update) | async-done | bytes 6291472 | tf_op jit(solution)/shard_map/while/body/eval_jaxpr/all_gather | solution.py:26
  727.2 8.2 %copy.7 = f32[24,8,8,1024]{3,2,1,0:T(8,128)S(1)} copy(f32[24,8,8,1024]{3,1,2,0:T(8,128)} %bitcast.40) | data formatting | bytes 12582912 | tf_op jit(solution)/shard_map/while
  737.6 4.4 select_dynamic-update-slice_fusion.2
  743.3 5.0 collective-permute-start
  (68 shorter events, 56.4 us)
Async XLA Ops:
  7.5 103.0 %all-gather.5.cloned.1.call-start = ((), (), s32[]{:S(2)}) async-start(), calls=%async_computation | async-start | bytes 7077888 | tf_op jit(solution)/shard_map/while/body/eval_jaxpr/all_gather | solution.py:26
  118.8 2.2 copy-start
  120.3 5.1 copy-start.1
  126.6 7.6 %collective-permute-start = (f32[256,192]{0,1:T(8,128)S(1)}, f32[256,192]{0,1:T(8,128)S(1)}, u32[]{:S(2)}, u32[]{:S(2)}) collective-permute-start(f32[256,192]{0,1:T(8,128)S(1)} %get-tuple-element.265), channel_id=1, source_target_pairs={{0,8},{8,16},{16,24},{1,9},{9,17},{17,25},{2,10},{10,18},{18,26},{... | collective-permute-start | bytes 589832 | tf_op jit(solution)/shard_map/while/body/eval_jaxpr/ppermute | solution.py:10
  134.2 99.9 %all-gather.5.cloned.1.call-start = ((), (), s32[]{:S(2)}) async-start(), calls=%async_computation | async-start | bytes 7077888 | tf_op jit(solution)/shard_map/while/body/eval_jaxpr/all_gather | solution.py:26
  242.3 2.2 copy-start
  243.8 5.1 copy-start.1
  250.2 7.6 %collective-permute-start = (f32[256,192]{0,1:T(8,128)S(1)}, f32[256,192]{0,1:T(8,128)S(1)}, u32[]{:S(2)}, u32[]{:S(2)}) collective-permute-start(f32[256,192]{0,1:T(8,128)S(1)} %get-tuple-element.265), channel_id=1, source_target_pairs={{0,8},{8,16},{16,24},{1,9},{9,17},{17,25},{2,10},{10,18},{18,26},{... | collective-permute-start | bytes 589832 | tf_op jit(solution)/shard_map/while/body/eval_jaxpr/ppermute | solution.py:10
  257.8 99.9 %all-gather.5.cloned.1.call-start = ((), (), s32[]{:S(2)}) async-start(), calls=%async_computation | async-start | bytes 7077888 | tf_op jit(solution)/shard_map/while/body/eval_jaxpr/all_gather | solution.py:26
  365.8 2.2 copy-start
  367.3 5.1 copy-start.1
  373.7 7.6 %collective-permute-start = (f32[256,192]{0,1:T(8,128)S(1)}, f32[256,192]{0,1:T(8,128)S(1)}, u32[]{:S(2)}, u32[]{:S(2)}) collective-permute-start(f32[256,192]{0,1:T(8,128)S(1)} %get-tuple-element.265), channel_id=1, source_target_pairs={{0,8},{8,16},{16,24},{1,9},{9,17},{17,25},{2,10},{10,18},{18,26},{... | collective-permute-start | bytes 589832 | tf_op jit(solution)/shard_map/while/body/eval_jaxpr/ppermute | solution.py:10
  381.3 99.5 %all-gather.5.cloned.1.call-start = ((), (), s32[]{:S(2)}) async-start(), calls=%async_computation | async-start | bytes 7077888 | tf_op jit(solution)/shard_map/while/body/eval_jaxpr/all_gather | solution.py:26
  489.0 2.2 copy-start
  490.5 5.1 copy-start.1
  496.9 7.6 %collective-permute-start = (f32[256,192]{0,1:T(8,128)S(1)}, f32[256,192]{0,1:T(8,128)S(1)}, u32[]{:S(2)}, u32[]{:S(2)}) collective-permute-start(f32[256,192]{0,1:T(8,128)S(1)} %get-tuple-element.265), channel_id=1, source_target_pairs={{0,8},{8,16},{16,24},{1,9},{9,17},{17,25},{2,10},{10,18},{18,26},{... | collective-permute-start | bytes 589832 | tf_op jit(solution)/shard_map/while/body/eval_jaxpr/ppermute | solution.py:10
  504.5 99.5 %all-gather.5.cloned.1.call-start = ((), (), s32[]{:S(2)}) async-start(), calls=%async_computation | async-start | bytes 7077888 | tf_op jit(solution)/shard_map/while/body/eval_jaxpr/all_gather | solution.py:26
  612.2 2.2 copy-start
  613.8 5.1 copy-start.1
  620.1 7.6 %collective-permute-start = (f32[256,192]{0,1:T(8,128)S(1)}, f32[256,192]{0,1:T(8,128)S(1)}, u32[]{:S(2)}, u32[]{:S(2)}) collective-permute-start(f32[256,192]{0,1:T(8,128)S(1)} %get-tuple-element.265), channel_id=1, source_target_pairs={{0,8},{8,16},{16,24},{1,9},{9,17},{17,25},{2,10},{10,18},{18,26},{... | collective-permute-start | bytes 589832 | tf_op jit(solution)/shard_map/while/body/eval_jaxpr/ppermute | solution.py:10
  627.7 99.5 %all-gather.5.cloned.1.call-start = ((), (), s32[]{:S(2)}) async-start(), calls=%async_computation | async-start | bytes 7077888 | tf_op jit(solution)/shard_map/while/body/eval_jaxpr/all_gather | solution.py:26
  735.4 2.2 copy-start
  737.0 5.1 copy-start.1
  743.3 7.6 %collective-permute-start = (f32[256,192]{0,1:T(8,128)S(1)}, f32[256,192]{0,1:T(8,128)S(1)}, u32[]{:S(2)}, u32[]{:S(2)}) collective-permute-start(f32[256,192]{0,1:T(8,128)S(1)} %get-tuple-element.265), channel_id=1, source_target_pairs={{0,8},{8,16},{16,24},{1,9},{9,17},{17,25},{2,10},{10,18},{18,26},{... | collective-permute-start | bytes 589832 | tf_op jit(solution)/shard_map/while/body/eval_jaxpr/ppermute | solution.py:10
  (2 other events, 3.0 us)
Sparse Core Ops, SparseCore 0:
  11.1 99.4 all-gather.4
  137.8 96.2 all-gather.4
  261.3 96.2 all-gather.4
  384.5 96.2 all-gather.4
  507.7 96.2 all-gather.4
  630.9 96.2 all-gather.4
